TPU v7x, 32 devices: a whole 2x2x4 slice. The times are simulated.
32 devices in a mesh: orb: 8 (over y, x, core), slab: 4 (over z).
Axes of the slice: x: 2, y: 2, z: 4, core: 2. Of those that a mesh axis runs over, the one named last changes fastest.
Arguments:
- pool: float32 [16, 32, 32, 128], P('orb', 'slab'), may hold values from -6 to 6
- target_row: int32 [8], P('orb'), may hold values from 0 to 1
- source_index: int32 [3], replicated, may hold values from 0 to 15
- metric: float32 [3, 32, 32, 128], P(None, 'slab'), may hold values from 0.3 to 3
- screening: float32 [32, 32, 128], P('slab'), may hold values from 0.05 to 4
Outputs:
- exchange: float32 [8, 32, 32, 128], P('orb', 'slab')
All inputs are finite; a program needn't handle non-finite values.
Results may differ from a plain program's by a relative error of at most 0.000096.
Values sent between devices are 32-bit elements; how exact they have to be, the bound alone decides.
No kernel may reach another device: no remote copies, remote signals or barrier semaphores. Data moves between devices by JAX's collectives and lax.ppermute only.
A program may use at most 64 MiB of HBM per device.

v0:
```python
import math
import jax
import jax.numpy as jnp
from jax import lax
from jax.sharding import PartitionSpec as P

NSRC = 3
SWEEPS = 6


def extended(cells, sides, width):
    for axis, dim in sides:
        count = lax.axis_size(axis)
        ends = count - 1
        head = lax.slice_in_dim(cells, 0, width, axis=dim)
        tail = lax.slice_in_dim(cells, cells.shape[dim] - width, cells.shape[dim], axis=dim)
        cells = jnp.concatenate(
            [
                lax.ppermute(tail, axis, [(i, (i + 1) % count) for i in range(ends)]),
                cells,
                lax.ppermute(head, axis, [((i + 1) % count, i) for i in range(ends)]),
            ],
            axis=dim,
        )
    return cells


def spread(value, axis, source):
    kept = jnp.where(lax.axis_index(axis) == source, value, 0).astype(value.dtype)
    return lax.psum(kept, axis)


def shifted(array, axis, by):
    size = lax.axis_size(axis)
    pairs = [(i, i + by) for i in range(size) if 0 <= i + by < size]
    return lax.ppermute(array, axis, pairs)


def lower_x(f):
    return jnp.concatenate([jnp.zeros_like(f[..., :1, :]), f[..., :-1, :]], axis=-2)


def upper_x(f):
    return jnp.concatenate([f[..., 1:, :], jnp.zeros_like(f[..., :1, :])], axis=-2)


def lower_y(f):
    return jnp.concatenate([jnp.zeros_like(f[..., :1]), f[..., :-1]], axis=-1)


def upper_y(f):
    return jnp.concatenate([f[..., 1:], jnp.zeros_like(f[..., :1])], axis=-1)


def step_sizes(count):
    return [
        1.0 / (1.025 + 0.975 * math.cos(math.pi * (2 * k + 1) / (2 * count))) for k in range(count)
    ]


def apply_rest(field, up_plane, down_plane, faces, diag):
    face_x, face_y, face_z, below_x, below_y, below_z = faces
    return (
        diag * field
        - face_z * up_plane
        - below_z * down_plane
        - face_x * upper_x(field)
        - below_x * lower_x(field)
        - face_y * upper_y(field)
        - below_y * lower_y(field)
    )


def sweep_rimmed(density, faces, diag, weights):
    field = weights[0] * density / diag
    for k in range(1, SWEEPS):
        padded = extended(field, (("slab", 1),), 1)
        image = apply_rest(field, padded[:, 2:], padded[:, :-2], faces, diag)
        field = field + weights[k] * (density - image) / diag
    return field


def shards(pool, target_row, source_index, metric, screening):
    held = pool.shape[0]
    weights = step_sizes(SWEEPS)
    copies = []
    for s in range(NSRC):
        which = source_index[s]
        mine = lax.dynamic_index_in_dim(pool, which % held, 0, keepdims=False)
        copies.append(spread(mine, "orb", which // held))
    sources = jnp.stack(copies)
    targets = jnp.take(pool, target_row, axis=0)
    face_x, face_y, face_z = (metric[0], metric[1], metric[2])
    last_plane = shifted(face_z[-1:], "slab", 1)
    below_z = jnp.concatenate([last_plane, face_z[:-1]], axis=0)
    below_x, below_y = (lower_x(face_x), lower_y(face_y))
    faces = (face_x, face_y, face_z, below_x, below_y, below_z)
    diag = screening + face_z + below_z + face_x + below_x + face_y + below_y
    density = targets[0][None] * sources
    fields = [sweep_rimmed(density[s : s + 1], faces, diag, weights) for s in range(NSRC)]
    field = jnp.concatenate(fields, axis=0)
    results = [jnp.sum(field * sources, axis=0)]
    return jnp.stack(results)


def solution(mesh):
    in_specs = (
        P("orb", "slab", None, None),
        P("orb"),
        P(),
        P(None, "slab", None, None),
        P("slab", None, None),
    )
    out_specs = P("orb", "slab", None, None)
    return jax.shard_map(shards, mesh=mesh, in_specs=in_specs, out_specs=out_specs, check_vma=False)
```

profile of v0, /device:TPU:24, one launch (start us, length us, event | category | flops | bytes accessed | tf_op | source)
XLA Modules:
  0.0 196.4 jit_solution(3746264836589793208)
XLA Ops:
  17.2 1.8 fusion.186
  20.1 55.9 %all-reduce.65.cloned.1.call-done = (f32[1,8,32,128]{3,2,1,0:T(8,128)}, f32[1,8,32,128]{3,2,1,0:T(8,128)}, f32[1,8,32,128]{3,2,1,0:T(8,128)}) async-done(((f32[1,8,32,128]{3,2,1,0:T(8,128)}, f32[1,8,32,128]{3,2,1,0:T(8,128)}, f32[1,8,32,128]{3,2,1,0:T(8,128)}), (f32[1,8,32,128]{3,2,1,0:T(8,128)}, f32[1,8,32,128]{3,2,1,0:T(8,128)}, f32[1,8,32,128]{3,2,1,0:T(8,128)})) %all-reduce.65.cloned.1.call-update) | async-done | bytes 393232 | tf_op jit(solution)/shard_map/psum | solution.py:30
  78.9 2.4 %collective-permute-start.1 = (f32[1,1,32,128]{3,2,1,0:T(8,128)S(1)}, f32[1,1,32,128]{3,2,1,0:T(8,128)S(1)}, u32[]{:S(2)}, u32[]{:S(2)}) collective-permute-start(f32[1,1,32,128]{3,2,1,0:T(8,128)S(1)} %get-tuple-element.59), channel_id=1, source_target_pairs={{1,0},{2,1},{3,2},{5,4},{6,5},{7,6},{9,8},{10,9},{11,10},{13,12},{... | collective-permute-start | bytes 49160 | tf_op jit(solution)/shard_map/ppermute | solution.py:21
  81.4 1.3 collective-permute-start.2
  82.8 4.2 %collective-permute-done.2 = f32[1,1,32,128]{3,2,1,0:T(8,128)S(1)} collective-permute-done((f32[1,1,32,128]{3,2,1,0:T(8,128)S(1)}, f32[1,1,32,128]{3,2,1,0:T(8,128)S(1)}, u32[]{:S(2)}, u32[]{:S(2)}) %collective-permute-start.2) | collective-permute-done | bytes 16416 | tf_op jit(solution)/shard_map/ppermute | solution.py:19
  87.3 2.4 %collective-permute-start.3 = (f32[1,1,32,128]{3,2,1,0:T(8,128)S(1)}, f32[1,1,32,128]{3,2,1,0:T(8,128)S(1)}, u32[]{:S(2)}, u32[]{:S(2)}) collective-permute-start(f32[1,1,32,128]{3,2,1,0:T(8,128)S(1)} %get-tuple-element.53), channel_id=1, source_target_pairs={{1,0},{2,1},{3,2},{5,4},{6,5},{7,6},{9,8},{10,9},{11,10},{13,12},{... | collective-permute-start | bytes 49160 | tf_op jit(solution)/shard_map/ppermute | solution.py:21
  89.7 1.3 collective-permute-start.4
  91.1 4.2 %collective-permute-done.4 = f32[1,1,32,128]{3,2,1,0:T(8,128)S(1)} collective-permute-done((f32[1,1,32,128]{3,2,1,0:T(8,128)S(1)}, f32[1,1,32,128]{3,2,1,0:T(8,128)S(1)}, u32[]{:S(2)}, u32[]{:S(2)}) %collective-permute-start.4) | collective-permute-done | bytes 16416 | tf_op jit(solution)/shard_map/ppermute | solution.py:19
  95.6 2.5 %collective-permute-start.5 = (f32[1,1,32,128]{3,2,1,0:T(8,128)S(1)}, f32[1,1,32,128]{3,2,1,0:T(8,128)S(1)}, u32[]{:S(2)}, u32[]{:S(2)}) collective-permute-start(f32[1,1,32,128]{3,2,1,0:T(8,128)S(1)} %get-tuple-element.47), channel_id=1, source_target_pairs={{1,0},{2,1},{3,2},{5,4},{6,5},{7,6},{9,8},{10,9},{11,10},{13,12},{... | collective-permute-start | bytes 49160 | tf_op jit(solution)/shard_map/ppermute | solution.py:21
  98.1 1.3 collective-permute-start.6
  99.5 4.2 %collective-permute-done.6 = f32[1,1,32,128]{3,2,1,0:T(8,128)S(1)} collective-permute-done((f32[1,1,32,128]{3,2,1,0:T(8,128)S(1)}, f32[1,1,32,128]{3,2,1,0:T(8,128)S(1)}, u32[]{:S(2)}, u32[]{:S(2)}) %collective-permute-start.6) | collective-permute-done | bytes 16416 | tf_op jit(solution)/shard_map/ppermute | solution.py:19
  104.0 1.9 collective-permute-start.7
  105.9 1.3 collective-permute-start.8
  107.3 4.2 %collective-permute-done.8 = f32[1,1,32,128]{3,2,1,0:T(8,128)S(1)} collective-permute-done((f32[1,1,32,128]{3,2,1,0:T(8,128)S(1)}, f32[1,1,32,128]{3,2,1,0:T(8,128)S(1)}, u32[]{:S(2)}, u32[]{:S(2)}) %collective-permute-start.8) | collective-permute-done | bytes 16416 | tf_op jit(solution)/shard_map/ppermute | solution.py:19
  111.9 1.9 collective-permute-start.11
  113.9 1.3 collective-permute-start.12
  115.2 1.3 collective-permute-start.10
  116.5 5.2 %collective-permute-start.9 = (f32[1,1,32,128]{3,2,1,0:T(8,128)S(1)}, f32[1,1,32,128]{3,2,1,0:T(8,128)S(1)}, u32[]{:S(2)}, u32[]{:S(2)}) collective-permute-start(f32[1,1,32,128]{3,2,1,0:T(8,128)S(1)} %get-tuple-element.35), channel_id=1, source_target_pairs={{1,0},{2,1},{3,2},{5,4},{6,5},{7,6},{9,8},{10,9},{11,10},{13,12},{... | collective-permute-start | bytes 49160 | tf_op jit(solution)/shard_map/ppermute | solution.py:21
  123.4 4.2 %collective-permute-start.13 = (f32[1,1,32,128]{3,2,1,0:T(8,128)S(1)}, f32[1,1,32,128]{3,2,1,0:T(8,128)S(1)}, u32[]{:S(2)}, u32[]{:S(2)}) collective-permute-start(f32[1,1,32,128]{3,2,1,0:T(8,128)S(1)} %get-tuple-element.83), channel_id=1, source_target_pairs={{1,0},{2,1},{3,2},{5,4},{6,5},{7,6},{9,8},{10,9},{11,10},{13,12},{... | collective-permute-start | bytes 49160 | tf_op jit(solution)/shard_map/ppermute | solution.py:21
  129.0 4.6 %collective-permute-start.21 = (f32[1,1,32,128]{3,2,1,0:T(8,128)S(1)}, f32[1,1,32,128]{3,2,1,0:T(8,128)S(1)}, u32[]{:S(2)}, u32[]{:S(2)}) collective-permute-start(f32[1,1,32,128]{3,2,1,0:T(8,128)S(1)} %get-tuple-element.119), channel_id=1, source_target_pairs={{1,0},{2,1},{3,2},{5,4},{6,5},{7,6},{9,8},{10,9},{11,10},{13,12},{... | collective-permute-start | bytes 49160 | tf_op jit(solution)/shard_map/ppermute | solution.py:21
  135.2 3.9 %collective-permute-done.22 = f32[1,1,32,128]{3,2,1,0:T(8,128)S(1)} collective-permute-done((f32[1,1,32,128]{3,2,1,0:T(8,128)S(1)}, f32[1,1,32,128]{3,2,1,0:T(8,128)S(1)}, u32[]{:S(2)}, u32[]{:S(2)}) %collective-permute-start.22) | collective-permute-done | bytes 16416 | tf_op jit(solution)/shard_map/ppermute | solution.py:19
  139.5 3.9 %collective-permute-start.15 = (f32[1,1,32,128]{3,2,1,0:T(8,128)S(1)}, f32[1,1,32,128]{3,2,1,0:T(8,128)S(1)}, u32[]{:S(2)}, u32[]{:S(2)}) collective-permute-start(f32[1,1,32,128]{3,2,1,0:T(8,128)S(1)} %get-tuple-element.77), channel_id=1, source_target_pairs={{1,0},{2,1},{3,2},{5,4},{6,5},{7,6},{9,8},{10,9},{11,10},{13,12},{... | collective-permute-start | bytes 49160 | tf_op jit(solution)/shard_map/ppermute | solution.py:21
  144.7 4.5 %collective-permute-start.23 = (f32[1,1,32,128]{3,2,1,0:T(8,128)S(1)}, f32[1,1,32,128]{3,2,1,0:T(8,128)S(1)}, u32[]{:S(2)}, u32[]{:S(2)}) collective-permute-start(f32[1,1,32,128]{3,2,1,0:T(8,128)S(1)} %get-tuple-element.113), channel_id=1, source_target_pairs={{1,0},{2,1},{3,2},{5,4},{6,5},{7,6},{9,8},{10,9},{11,10},{13,12},{... | collective-permute-start | bytes 49160 | tf_op jit(solution)/shard_map/ppermute | solution.py:21
  151.0 3.9 %collective-permute-done.24 = f32[1,1,32,128]{3,2,1,0:T(8,128)S(1)} collective-permute-done((f32[1,1,32,128]{3,2,1,0:T(8,128)S(1)}, f32[1,1,32,128]{3,2,1,0:T(8,128)S(1)}, u32[]{:S(2)}, u32[]{:S(2)}) %collective-permute-start.24) | collective-permute-done | bytes 16416 | tf_op jit(solution)/shard_map/ppermute | solution.py:19
  155.3 1.9 collective-permute-start.17
  157.2 1.3 collective-permute-start.18
  158.5 4.5 %collective-permute-start.25 = (f32[1,1,32,128]{3,2,1,0:T(8,128)S(1)}, f32[1,1,32,128]{3,2,1,0:T(8,128)S(1)}, u32[]{:S(2)}, u32[]{:S(2)}) collective-permute-start(f32[1,1,32,128]{3,2,1,0:T(8,128)S(1)} %get-tuple-element.107), channel_id=1, source_target_pairs={{1,0},{2,1},{3,2},{5,4},{6,5},{7,6},{9,8},{10,9},{11,10},{13,12},{... | collective-permute-start | bytes 49160 | tf_op jit(solution)/shard_map/ppermute | solution.py:21
  164.7 4.0 %collective-permute-done.26 = f32[1,1,32,128]{3,2,1,0:T(8,128)S(1)} collective-permute-done((f32[1,1,32,128]{3,2,1,0:T(8,128)S(1)}, f32[1,1,32,128]{3,2,1,0:T(8,128)S(1)}, u32[]{:S(2)}, u32[]{:S(2)}) %collective-permute-start.26) | collective-permute-done | bytes 16416 | tf_op jit(solution)/shard_map/ppermute | solution.py:19
  169.0 1.9 collective-permute-start.27
  172.3 4.5 %collective-permute-start.19 = (f32[1,1,32,128]{3,2,1,0:T(8,128)S(1)}, f32[1,1,32,128]{3,2,1,0:T(8,128)S(1)}, u32[]{:S(2)}, u32[]{:S(2)}) collective-permute-start(f32[1,1,32,128]{3,2,1,0:T(8,128)S(1)} %get-tuple-element.65), channel_id=1, source_target_pairs={{1,0},{2,1},{3,2},{5,4},{6,5},{7,6},{9,8},{10,9},{11,10},{13,12},{... | collective-permute-start | bytes 49160 | tf_op jit(solution)/shard_map/ppermute | solution.py:21
  178.4 4.5 %collective-permute-start.29 = (f32[1,1,32,128]{3,2,1,0:T(8,128)S(1)}, f32[1,1,32,128]{3,2,1,0:T(8,128)S(1)}, u32[]{:S(2)}, u32[]{:S(2)}) collective-permute-start(f32[1,1,32,128]{3,2,1,0:T(8,128)S(1)} %get-tuple-element.95), channel_id=1, source_target_pairs={{1,0},{2,1},{3,2},{5,4},{6,5},{7,6},{9,8},{10,9},{11,10},{13,12},{... | collective-permute-start | bytes 49160 | tf_op jit(solution)/shard_map/ppermute | solution.py:21
  184.6 4.0 %collective-permute-done.30 = f32[1,1,32,128]{3,2,1,0:T(8,128)S(1)} collective-permute-done((f32[1,1,32,128]{3,2,1,0:T(8,128)S(1)}, f32[1,1,32,128]{3,2,1,0:T(8,128)S(1)}, u32[]{:S(2)}, u32[]{:S(2)}) %collective-permute-start.30) | collective-permute-done | bytes 16416 | tf_op jit(solution)/shard_map/ppermute | solution.py:19
  (112 shorter events, 23.6 us)
Async XLA Ops:
  6.5 69.4 %all-reduce.65.cloned.1.call-start = ((), (), s32[]{:S(2)}) async-start(), calls=%async_computation | async-start | bytes 786432 | tf_op jit(solution)/shard_map/psum | solution.py:30
  7.3 70.6 %collective-permute-start = (f32[1,32,128]{2,1,0:T(8,128)S(1)}, f32[1,32,128]{2,1,0:T(8,128)S(1)}, u32[]{:S(2)}, u32[]{:S(2)}) collective-permute-start(f32[1,32,128]{2,1,0:T(8,128)S(1)} %slice_bitcast_fusion.1), channel_id=1, source_target_pairs={{0,1},{1,2},{2,3},{4,5},{5,6},{6,7},{8,9},{9,10},{10,11},{12,13},{... | collective-permute-start | bytes 49160 | tf_op jit(solution)/shard_map/ppermute | solution.py:36
  78.9 3.9 %collective-permute-start.1 = (f32[1,1,32,128]{3,2,1,0:T(8,128)S(1)}, f32[1,1,32,128]{3,2,1,0:T(8,128)S(1)}, u32[]{:S(2)}, u32[]{:S(2)}) collective-permute-start(f32[1,1,32,128]{3,2,1,0:T(8,128)S(1)} %get-tuple-element.59), channel_id=1, source_target_pairs={{1,0},{2,1},{3,2},{5,4},{6,5},{7,6},{9,8},{10,9},{11,10},{13,12},{... | collective-permute-start | bytes 49160 | tf_op jit(solution)/shard_map/ppermute | solution.py:21
  81.4 5.6 %collective-permute-start.2 = (f32[1,1,32,128]{3,2,1,0:T(8,128)S(1)}, f32[1,1,32,128]{3,2,1,0:T(8,128)S(1)}, u32[]{:S(2)}, u32[]{:S(2)}) collective-permute-start(f32[1,1,32,128]{3,2,1,0:T(8,128)S(1)} %get-tuple-element.60), channel_id=1, source_target_pairs={{0,1},{1,2},{2,3},{4,5},{5,6},{6,7},{8,9},{9,10},{10,11},{12,13},{... | collective-permute-start | bytes 49160 | tf_op jit(solution)/shard_map/ppermute | solution.py:19
  87.3 3.9 %collective-permute-start.3 = (f32[1,1,32,128]{3,2,1,0:T(8,128)S(1)}, f32[1,1,32,128]{3,2,1,0:T(8,128)S(1)}, u32[]{:S(2)}, u32[]{:S(2)}) collective-permute-start(f32[1,1,32,128]{3,2,1,0:T(8,128)S(1)} %get-tuple-element.53), channel_id=1, source_target_pairs={{1,0},{2,1},{3,2},{5,4},{6,5},{7,6},{9,8},{10,9},{11,10},{13,12},{... | collective-permute-start | bytes 49160 | tf_op jit(solution)/shard_map/ppermute | solution.py:21
  89.7 5.6 %collective-permute-start.4 = (f32[1,1,32,128]{3,2,1,0:T(8,128)S(1)}, f32[1,1,32,128]{3,2,1,0:T(8,128)S(1)}, u32[]{:S(2)}, u32[]{:S(2)}) collective-permute-start(f32[1,1,32,128]{3,2,1,0:T(8,128)S(1)} %get-tuple-element.54), channel_id=1, source_target_pairs={{0,1},{1,2},{2,3},{4,5},{5,6},{6,7},{8,9},{9,10},{10,11},{12,13},{... | collective-permute-start | bytes 49160 | tf_op jit(solution)/shard_map/ppermute | solution.py:19
  95.6 3.9 %collective-permute-start.5 = (f32[1,1,32,128]{3,2,1,0:T(8,128)S(1)}, f32[1,1,32,128]{3,2,1,0:T(8,128)S(1)}, u32[]{:S(2)}, u32[]{:S(2)}) collective-permute-start(f32[1,1,32,128]{3,2,1,0:T(8,128)S(1)} %get-tuple-element.47), channel_id=1, source_target_pairs={{1,0},{2,1},{3,2},{5,4},{6,5},{7,6},{9,8},{10,9},{11,10},{13,12},{... | collective-permute-start | bytes 49160 | tf_op jit(solution)/shard_map/ppermute | solution.py:21
  98.1 5.6 %collective-permute-start.6 = (f32[1,1,32,128]{3,2,1,0:T(8,128)S(1)}, f32[1,1,32,128]{3,2,1,0:T(8,128)S(1)}, u32[]{:S(2)}, u32[]{:S(2)}) collective-permute-start(f32[1,1,32,128]{3,2,1,0:T(8,128)S(1)} %get-tuple-element.48), channel_id=1, source_target_pairs={{0,1},{1,2},{2,3},{4,5},{5,6},{6,7},{8,9},{9,10},{10,11},{12,13},{... | collective-permute-start | bytes 49160 | tf_op jit(solution)/shard_map/ppermute | solution.py:19
  104.0 3.4 %collective-permute-start.7 = (f32[1,1,32,128]{3,2,1,0:T(8,128)S(1)}, f32[1,1,32,128]{3,2,1,0:T(8,128)S(1)}, u32[]{:S(2)}, u32[]{:S(2)}) collective-permute-start(f32[1,1,32,128]{3,2,1,0:T(8,128)S(1)} %get-tuple-element.41), channel_id=1, source_target_pairs={{1,0},{2,1},{3,2},{5,4},{6,5},{7,6},{9,8},{10,9},{11,10},{13,12},{... | collective-permute-start | bytes 49160 | tf_op jit(solution)/shard_map/ppermute | solution.py:21
  105.9 5.6 %collective-permute-start.8 = (f32[1,1,32,128]{3,2,1,0:T(8,128)S(1)}, f32[1,1,32,128]{3,2,1,0:T(8,128)S(1)}, u32[]{:S(2)}, u32[]{:S(2)}) collective-permute-start(f32[1,1,32,128]{3,2,1,0:T(8,128)S(1)} %get-tuple-element.42), channel_id=1, source_target_pairs={{0,1},{1,2},{2,3},{4,5},{5,6},{6,7},{8,9},{9,10},{10,11},{12,13},{... | collective-permute-start | bytes 49160 | tf_op jit(solution)/shard_map/ppermute | solution.py:19
  111.9 9.7 %collective-permute-start.11 = (f32[1,1,32,128]{3,2,1,0:T(8,128)S(1)}, f32[1,1,32,128]{3,2,1,0:T(8,128)S(1)}, u32[]{:S(2)}, u32[]{:S(2)}) collective-permute-start(f32[1,1,32,128]{3,2,1,0:T(8,128)S(1)} %get-tuple-element.89), channel_id=1, source_target_pairs={{1,0},{2,1},{3,2},{5,4},{6,5},{7,6},{9,8},{10,9},{11,10},{13,12},{... | collective-permute-start | bytes 49160 | tf_op jit(solution)/shard_map/ppermute | solution.py:21
  113.9 7.8 %collective-permute-start.12 = (f32[1,1,32,128]{3,2,1,0:T(8,128)S(1)}, f32[1,1,32,128]{3,2,1,0:T(8,128)S(1)}, u32[]{:S(2)}, u32[]{:S(2)}) collective-permute-start(f32[1,1,32,128]{3,2,1,0:T(8,128)S(1)} %get-tuple-element.90), channel_id=1, source_target_pairs={{0,1},{1,2},{2,3},{4,5},{5,6},{6,7},{8,9},{9,10},{10,11},{12,13},{... | collective-permute-start | bytes 49160 | tf_op jit(solution)/shard_map/ppermute | solution.py:19
  115.2 6.9 %collective-permute-start.10 = (f32[1,1,32,128]{3,2,1,0:T(8,128)S(1)}, f32[1,1,32,128]{3,2,1,0:T(8,128)S(1)}, u32[]{:S(2)}, u32[]{:S(2)}) collective-permute-start(f32[1,1,32,128]{3,2,1,0:T(8,128)S(1)} %get-tuple-element.36), channel_id=1, source_target_pairs={{0,1},{1,2},{2,3},{4,5},{5,6},{6,7},{8,9},{9,10},{10,11},{12,13},{... | collective-permute-start | bytes 49160 | tf_op jit(solution)/shard_map/ppermute | solution.py:19
  116.5 6.6 %collective-permute-start.9 = (f32[1,1,32,128]{3,2,1,0:T(8,128)S(1)}, f32[1,1,32,128]{3,2,1,0:T(8,128)S(1)}, u32[]{:S(2)}, u32[]{:S(2)}) collective-permute-start(f32[1,1,32,128]{3,2,1,0:T(8,128)S(1)} %get-tuple-element.35), channel_id=1, source_target_pairs={{1,0},{2,1},{3,2},{5,4},{6,5},{7,6},{9,8},{10,9},{11,10},{13,12},{... | collective-permute-start | bytes 49160 | tf_op jit(solution)/shard_map/ppermute | solution.py:21
  123.4 11.4 %collective-permute-start.13 = (f32[1,1,32,128]{3,2,1,0:T(8,128)S(1)}, f32[1,1,32,128]{3,2,1,0:T(8,128)S(1)}, u32[]{:S(2)}, u32[]{:S(2)}) collective-permute-start(f32[1,1,32,128]{3,2,1,0:T(8,128)S(1)} %get-tuple-element.83), channel_id=1, source_target_pairs={{1,0},{2,1},{3,2},{5,4},{6,5},{7,6},{9,8},{10,9},{11,10},{13,12},{... | collective-permute-start | bytes 49160 | tf_op jit(solution)/shard_map/ppermute | solution.py:21
  127.6 7.2 %collective-permute-start.14 = (f32[1,1,32,128]{3,2,1,0:T(8,128)S(1)}, f32[1,1,32,128]{3,2,1,0:T(8,128)S(1)}, u32[]{:S(2)}, u32[]{:S(2)}) collective-permute-start(f32[1,1,32,128]{3,2,1,0:T(8,128)S(1)} %get-tuple-element.84), channel_id=1, source_target_pairs={{0,1},{1,2},{2,3},{4,5},{5,6},{6,7},{8,9},{9,10},{10,11},{12,13},{... | collective-permute-start | bytes 49160 | tf_op jit(solution)/shard_map/ppermute | solution.py:19
  129.0 6.2 %collective-permute-start.21 = (f32[1,1,32,128]{3,2,1,0:T(8,128)S(1)}, f32[1,1,32,128]{3,2,1,0:T(8,128)S(1)}, u32[]{:S(2)}, u32[]{:S(2)}) collective-permute-start(f32[1,1,32,128]{3,2,1,0:T(8,128)S(1)} %get-tuple-element.119), channel_id=1, source_target_pairs={{1,0},{2,1},{3,2},{5,4},{6,5},{7,6},{9,8},{10,9},{11,10},{13,12},{... | collective-permute-start | bytes 49160 | tf_op jit(solution)/shard_map/ppermute | solution.py:21
  133.5 5.6 %collective-permute-start.22 = (f32[1,1,32,128]{3,2,1,0:T(8,128)S(1)}, f32[1,1,32,128]{3,2,1,0:T(8,128)S(1)}, u32[]{:S(2)}, u32[]{:S(2)}) collective-permute-start(f32[1,1,32,128]{3,2,1,0:T(8,128)S(1)} %get-tuple-element.120), channel_id=1, source_target_pairs={{0,1},{1,2},{2,3},{4,5},{5,6},{6,7},{8,9},{9,10},{10,11},{12,13},{... | collective-permute-start | bytes 49160 | tf_op jit(solution)/shard_map/ppermute | solution.py:19
  139.5 11.1 %collective-permute-start.15 = (f32[1,1,32,128]{3,2,1,0:T(8,128)S(1)}, f32[1,1,32,128]{3,2,1,0:T(8,128)S(1)}, u32[]{:S(2)}, u32[]{:S(2)}) collective-permute-start(f32[1,1,32,128]{3,2,1,0:T(8,128)S(1)} %get-tuple-element.77), channel_id=1, source_target_pairs={{1,0},{2,1},{3,2},{5,4},{6,5},{7,6},{9,8},{10,9},{11,10},{13,12},{... | collective-permute-start | bytes 49160 | tf_op jit(solution)/shard_map/ppermute | solution.py:21
  143.4 7.2 %collective-permute-start.16 = (f32[1,1,32,128]{3,2,1,0:T(8,128)S(1)}, f32[1,1,32,128]{3,2,1,0:T(8,128)S(1)}, u32[]{:S(2)}, u32[]{:S(2)}) collective-permute-start(f32[1,1,32,128]{3,2,1,0:T(8,128)S(1)} %get-tuple-element.78), channel_id=1, source_target_pairs={{0,1},{1,2},{2,3},{4,5},{5,6},{6,7},{8,9},{9,10},{10,11},{12,13},{... | collective-permute-start | bytes 49160 | tf_op jit(solution)/shard_map/ppermute | solution.py:19
  144.7 6.2 %collective-permute-start.23 = (f32[1,1,32,128]{3,2,1,0:T(8,128)S(1)}, f32[1,1,32,128]{3,2,1,0:T(8,128)S(1)}, u32[]{:S(2)}, u32[]{:S(2)}) collective-permute-start(f32[1,1,32,128]{3,2,1,0:T(8,128)S(1)} %get-tuple-element.113), channel_id=1, source_target_pairs={{1,0},{2,1},{3,2},{5,4},{6,5},{7,6},{9,8},{10,9},{11,10},{13,12},{... | collective-permute-start | bytes 49160 | tf_op jit(solution)/shard_map/ppermute | solution.py:21
  149.3 5.6 %collective-permute-start.24 = (f32[1,1,32,128]{3,2,1,0:T(8,128)S(1)}, f32[1,1,32,128]{3,2,1,0:T(8,128)S(1)}, u32[]{:S(2)}, u32[]{:S(2)}) collective-permute-start(f32[1,1,32,128]{3,2,1,0:T(8,128)S(1)} %get-tuple-element.114), channel_id=1, source_target_pairs={{0,1},{1,2},{2,3},{4,5},{5,6},{6,7},{8,9},{9,10},{10,11},{12,13},{... | collective-permute-start | bytes 49160 | tf_op jit(solution)/shard_map/ppermute | solution.py:19
  155.3 9.1 %collective-permute-start.17 = (f32[1,1,32,128]{3,2,1,0:T(8,128)S(1)}, f32[1,1,32,128]{3,2,1,0:T(8,128)S(1)}, u32[]{:S(2)}, u32[]{:S(2)}) collective-permute-start(f32[1,1,32,128]{3,2,1,0:T(8,128)S(1)} %get-tuple-element.71), channel_id=1, source_target_pairs={{1,0},{2,1},{3,2},{5,4},{6,5},{7,6},{9,8},{10,9},{11,10},{13,12},{... | collective-permute-start | bytes 49160 | tf_op jit(solution)/shard_map/ppermute | solution.py:21
  157.2 7.2 %collective-permute-start.18 = (f32[1,1,32,128]{3,2,1,0:T(8,128)S(1)}, f32[1,1,32,128]{3,2,1,0:T(8,128)S(1)}, u32[]{:S(2)}, u32[]{:S(2)}) collective-permute-start(f32[1,1,32,128]{3,2,1,0:T(8,128)S(1)} %get-tuple-element.72), channel_id=1, source_target_pairs={{0,1},{1,2},{2,3},{4,5},{5,6},{6,7},{8,9},{9,10},{10,11},{12,13},{... | collective-permute-start | bytes 49160 | tf_op jit(solution)/shard_map/ppermute | solution.py:19
  158.5 6.2 %collective-permute-start.25 = (f32[1,1,32,128]{3,2,1,0:T(8,128)S(1)}, f32[1,1,32,128]{3,2,1,0:T(8,128)S(1)}, u32[]{:S(2)}, u32[]{:S(2)}) collective-permute-start(f32[1,1,32,128]{3,2,1,0:T(8,128)S(1)} %get-tuple-element.107), channel_id=1, source_target_pairs={{1,0},{2,1},{3,2},{5,4},{6,5},{7,6},{9,8},{10,9},{11,10},{13,12},{... | collective-permute-start | bytes 49160 | tf_op jit(solution)/shard_map/ppermute | solution.py:21
  163.1 5.6 %collective-permute-start.26 = (f32[1,1,32,128]{3,2,1,0:T(8,128)S(1)}, f32[1,1,32,128]{3,2,1,0:T(8,128)S(1)}, u32[]{:S(2)}, u32[]{:S(2)}) collective-permute-start(f32[1,1,32,128]{3,2,1,0:T(8,128)S(1)} %get-tuple-element.108), channel_id=1, source_target_pairs={{0,1},{1,2},{2,3},{4,5},{5,6},{6,7},{8,9},{9,10},{10,11},{12,13},{... | collective-permute-start | bytes 49160 | tf_op jit(solution)/shard_map/ppermute | solution.py:19
  169.0 9.1 %collective-permute-start.27 = (f32[1,1,32,128]{3,2,1,0:T(8,128)S(1)}, f32[1,1,32,128]{3,2,1,0:T(8,128)S(1)}, u32[]{:S(2)}, u32[]{:S(2)}) collective-permute-start(f32[1,1,32,128]{3,2,1,0:T(8,128)S(1)} %get-tuple-element.101), channel_id=1, source_target_pairs={{1,0},{2,1},{3,2},{5,4},{6,5},{7,6},{9,8},{10,9},{11,10},{13,12},{... | collective-permute-start | bytes 49160 | tf_op jit(solution)/shard_map/ppermute | solution.py:21
  171.0 7.2 %collective-permute-start.28 = (f32[1,1,32,128]{3,2,1,0:T(8,128)S(1)}, f32[1,1,32,128]{3,2,1,0:T(8,128)S(1)}, u32[]{:S(2)}, u32[]{:S(2)}) collective-permute-start(f32[1,1,32,128]{3,2,1,0:T(8,128)S(1)} %get-tuple-element.102), channel_id=1, source_target_pairs={{0,1},{1,2},{2,3},{4,5},{5,6},{6,7},{8,9},{9,10},{10,11},{12,13},{... | collective-permute-start | bytes 49160 | tf_op jit(solution)/shard_map/ppermute | solution.py:19
  172.3 12.0 %collective-permute-start.19 = (f32[1,1,32,128]{3,2,1,0:T(8,128)S(1)}, f32[1,1,32,128]{3,2,1,0:T(8,128)S(1)}, u32[]{:S(2)}, u32[]{:S(2)}) collective-permute-start(f32[1,1,32,128]{3,2,1,0:T(8,128)S(1)} %get-tuple-element.65), channel_id=1, source_target_pairs={{1,0},{2,1},{3,2},{5,4},{6,5},{7,6},{9,8},{10,9},{11,10},{13,12},{... | collective-permute-start | bytes 49160 | tf_op jit(solution)/shard_map/ppermute | solution.py:21
  176.8 7.5 %collective-permute-start.20 = (f32[1,1,32,128]{3,2,1,0:T(8,128)S(1)}, f32[1,1,32,128]{3,2,1,0:T(8,128)S(1)}, u32[]{:S(2)}, u32[]{:S(2)}) collective-permute-start(f32[1,1,32,128]{3,2,1,0:T(8,128)S(1)} %get-tuple-element.66), channel_id=1, source_target_pairs={{0,1},{1,2},{2,3},{4,5},{5,6},{6,7},{8,9},{9,10},{10,11},{12,13},{... | collective-permute-start | bytes 49160 | tf_op jit(solution)/shard_map/ppermute | solution.py:19
  178.4 6.2 %collective-permute-start.29 = (f32[1,1,32,128]{3,2,1,0:T(8,128)S(1)}, f32[1,1,32,128]{3,2,1,0:T(8,128)S(1)}, u32[]{:S(2)}, u32[]{:S(2)}) collective-permute-start(f32[1,1,32,128]{3,2,1,0:T(8,128)S(1)} %get-tuple-element.95), channel_id=1, source_target_pairs={{1,0},{2,1},{3,2},{5,4},{6,5},{7,6},{9,8},{10,9},{11,10},{13,12},{... | collective-permute-start | bytes 49160 | tf_op jit(solution)/shard_map/ppermute | solution.py:21
  183.0 5.6 %collective-permute-start.30 = (f32[1,1,32,128]{3,2,1,0:T(8,128)S(1)}, f32[1,1,32,128]{3,2,1,0:T(8,128)S(1)}, u32[]{:S(2)}, u32[]{:S(2)}) collective-permute-start(f32[1,1,32,128]{3,2,1,0:T(8,128)S(1)} %get-tuple-element.96), channel_id=1, source_target_pairs={{0,1},{1,2},{2,3},{4,5},{5,6},{6,7},{8,9},{9,10},{10,11},{12,13},{... | collective-permute-start | bytes 49160 | tf_op jit(solution)/shard_map/ppermute | solution.py:19
  (5 other events, 5.8 us)
Sparse Core Ops, SparseCore 0:
  19.2 56.7 all-reduce.64
where the time goes:
time: 198 us; the launch traced here: 196 us
  waiting for transfers between devices  89.7 us (45%)
  starting transfers between devices  71.7 us (36%)
  between operations  22.2 us (11%)
  local copies, waits for them, and re-layouts  6.69 us (3%)
  other arithmetic  5.98 us (3%)
    psum x1, waiting for transfers between devices, spread(): return lax.psum(kept, axis)  55.9 us
    ppermute x15, starting transfers between devices, extended(): lax.ppermute(head, axis, [((i + 1) % count, i) for i in range(ends)])  51.1 us
    ppermute x15, waiting for transfers between devices, extended(): lax.ppermute(tail, axis, [(i, (i + 1) % count) for i in range(ends)])  32.7 us
    ppermute x15, starting transfers between devices, extended(): lax.ppermute(tail, axis, [(i, (i + 1) % count) for i in range(ends)])  19.4 us
  transfers between devices with their start and end apart: 32, of which 10 were waited for; matrix products, arithmetic and copies ran while one was open for 3% of the time, Pallas kernels for 0%

commit v1 on v0

--- a/solution.py
+++ b/solution.py
@@ -3,6 +3,7 @@
 import jax.numpy as jnp
 from jax import lax
 from jax.sharding import PartitionSpec as P
+from jax.lax import all_gather
 
 NSRC = 3
 SWEEPS = 6
@@ -27,7 +28,7 @@
 
 def spread(value, axis, source):
     kept = jnp.where(lax.axis_index(axis) == source, value, 0).astype(value.dtype)
-    return lax.psum(kept, axis)
+    return all_gather(kept, axis_name=axis).sum(axis=0)
 
 
 def shifted(array, axis, by):

time: 198 us -> 214 us (1.081)
  waiting for transfers between devices: 89.7 us -> 105 us
  other arithmetic: 5.98 us -> 9.91 us
  local copies, waits for them, and re-layouts: 6.69 us -> 3.92 us
    all_gather x0 -> x3, waiting for transfers between devices: none -> 70 us  [spread(): return all_gather(kept, axis_name=axis).sum(axis=0)]
    psum x1 -> x0, waiting for transfers between devices: 55.9 us -> none  [spread(): return lax.psum(kept, axis)]
    reduce_sum x0 -> x3, other arithmetic: none -> 3.92 us  [spread(): return all_gather(kept, axis_name=axis).sum(axis=0)]
    unnamed x12 -> x4, local copies, waits for them, and re-layouts: 3.67 us -> 0.85 us
  transfers between devices with their start and end apart: 32 -> 34, of which waited for: 10 -> 12; matrix products, arithmetic and copies ran while one was open for 3% -> 3% of each run, Pallas kernels for 0% -> 0%
where the time goes in v1:
time: 214 us; the launch traced here: 213 us
  waiting for transfers between devices  105 us (49%)
  starting transfers between devices  71.6 us (33%)
  between operations  22.2 us (10%)
  other arithmetic  9.91 us (5%)
  local copies, waits for them, and re-layouts  3.92 us (2%)
    all_gather x3, waiting for transfers between devices, spread(): return all_gather(kept, axis_name=axis).sum(axis=0)  70 us
    ppermute x15, starting transfers between devices, extended(): lax.ppermute(head, axis, [((i + 1) % count, i) for i in range(ends)])  50.8 us
    ppermute x15, waiting for transfers between devices, extended(): lax.ppermute(tail, axis, [(i, (i + 1) % count) for i in range(ends)])  32.9 us
    ppermute x15, starting transfers between devices, extended(): lax.ppermute(tail, axis, [(i, (i + 1) % count) for i in range(ends)])  19.4 us
  transfers between devices with their start and end apart: 34, of which 12 were waited for; matrix products, arithmetic and copies ran while one was open for 3% of the time, Pallas kernels for 0%

profile of v1, /device:TPU:24, one launch (start us, length us, event | category | flops | bytes accessed | tf_op | source)
XLA Modules:
  0.0 213.1 jit_solution(18259972495252376488)
XLA Ops:
  6.5 1.4 fusion.234
  16.3 1.9 fusion.187
  21.0 21.8 %all-gather.4.cloned.1.call-done = f32[8,8,32,128]{3,2,1,0:T(8,128)} async-done(((f32[1,8,32,128]{3,2,1,0:T(8,128)}), f32[8,8,32,128]{3,2,1,0:T(8,128)}) %all-gather.4.cloned.1.call-update) | async-done | bytes 1048592 | tf_op jit(solution)/shard_map/all_gather | solution.py:31
  42.8 1.3 reduce_sum.36
  44.1 24.1 %all-gather.6.cloned.1.call-done = f32[8,8,32,128]{3,2,1,0:T(8,128)} async-done(((f32[1,8,32,128]{3,2,1,0:T(8,128)}), f32[8,8,32,128]{3,2,1,0:T(8,128)}) %all-gather.6.cloned.1.call-update) | async-done | bytes 1048592 | tf_op jit(solution)/shard_map/all_gather | solution.py:31
  68.2 1.3 reduce_sum.37
  69.5 24.1 %all-gather.8.cloned.1.call-done = f32[8,8,32,128]{3,2,1,0:T(8,128)} async-done(((f32[1,8,32,128]{3,2,1,0:T(8,128)}), f32[8,8,32,128]{3,2,1,0:T(8,128)}) %all-gather.8.cloned.1.call-update) | async-done | bytes 1048592 | tf_op jit(solution)/shard_map/all_gather | solution.py:31
  93.6 1.3 reduce_sum.38
  96.0 2.4 %collective-permute-start.1 = (f32[1,1,32,128]{3,2,1,0:T(8,128)S(1)}, f32[1,1,32,128]{3,2,1,0:T(8,128)S(1)}, u32[]{:S(2)}, u32[]{:S(2)}) collective-permute-start(f32[1,1,32,128]{3,2,1,0:T(8,128)S(1)} %get-tuple-element.56), channel_id=1, source_target_pairs={{1,0},{2,1},{3,2},{5,4},{6,5},{7,6},{9,8},{10,9},{11,10},{13,12},{... | collective-permute-start | bytes 49160 | tf_op jit(solution)/shard_map/ppermute | solution.py:22
  99.8 4.2 %collective-permute-done.2 = f32[1,1,32,128]{3,2,1,0:T(8,128)S(1)} collective-permute-done((f32[1,1,32,128]{3,2,1,0:T(8,128)S(1)}, f32[1,1,32,128]{3,2,1,0:T(8,128)S(1)}, u32[]{:S(2)}, u32[]{:S(2)}) %collective-permute-start.2) | collective-permute-done | bytes 16416 | tf_op jit(solution)/shard_map/ppermute | solution.py:20
  104.3 2.4 %collective-permute-start.3 = (f32[1,1,32,128]{3,2,1,0:T(8,128)S(1)}, f32[1,1,32,128]{3,2,1,0:T(8,128)S(1)}, u32[]{:S(2)}, u32[]{:S(2)}) collective-permute-start(f32[1,1,32,128]{3,2,1,0:T(8,128)S(1)} %get-tuple-element.50), channel_id=1, source_target_pairs={{1,0},{2,1},{3,2},{5,4},{6,5},{7,6},{9,8},{10,9},{11,10},{13,12},{... | collective-permute-start | bytes 49160 | tf_op jit(solution)/shard_map/ppermute | solution.py:22
  108.2 4.2 %collective-permute-done.4 = f32[1,1,32,128]{3,2,1,0:T(8,128)S(1)} collective-permute-done((f32[1,1,32,128]{3,2,1,0:T(8,128)S(1)}, f32[1,1,32,128]{3,2,1,0:T(8,128)S(1)}, u32[]{:S(2)}, u32[]{:S(2)}) %collective-permute-start.4) | collective-permute-done | bytes 16416 | tf_op jit(solution)/shard_map/ppermute | solution.py:20
  112.7 2.4 %collective-permute-start.5 = (f32[1,1,32,128]{3,2,1,0:T(8,128)S(1)}, f32[1,1,32,128]{3,2,1,0:T(8,128)S(1)}, u32[]{:S(2)}, u32[]{:S(2)}) collective-permute-start(f32[1,1,32,128]{3,2,1,0:T(8,128)S(1)} %get-tuple-element.44), channel_id=1, source_target_pairs={{1,0},{2,1},{3,2},{5,4},{6,5},{7,6},{9,8},{10,9},{11,10},{13,12},{... | collective-permute-start | bytes 49160 | tf_op jit(solution)/shard_map/ppermute | solution.py:22
  116.5 4.2 %collective-permute-done.6 = f32[1,1,32,128]{3,2,1,0:T(8,128)S(1)} collective-permute-done((f32[1,1,32,128]{3,2,1,0:T(8,128)S(1)}, f32[1,1,32,128]{3,2,1,0:T(8,128)S(1)}, u32[]{:S(2)}, u32[]{:S(2)}) %collective-permute-start.6) | collective-permute-done | bytes 16416 | tf_op jit(solution)/shard_map/ppermute | solution.py:20
  121.0 1.9 collective-permute-start.7
  124.4 4.2 %collective-permute-done.8 = f32[1,1,32,128]{3,2,1,0:T(8,128)S(1)} collective-permute-done((f32[1,1,32,128]{3,2,1,0:T(8,128)S(1)}, f32[1,1,32,128]{3,2,1,0:T(8,128)S(1)}, u32[]{:S(2)}, u32[]{:S(2)}) %collective-permute-start.8) | collective-permute-done | bytes 16416 | tf_op jit(solution)/shard_map/ppermute | solution.py:20
  129.0 1.9 collective-permute-start.11
  130.9 1.3 collective-permute-start.12
  133.5 5.2 %collective-permute-start.9 = (f32[1,1,32,128]{3,2,1,0:T(8,128)S(1)}, f32[1,1,32,128]{3,2,1,0:T(8,128)S(1)}, u32[]{:S(2)}, u32[]{:S(2)}) collective-permute-start(f32[1,1,32,128]{3,2,1,0:T(8,128)S(1)} %get-tuple-element.32), channel_id=1, source_target_pairs={{1,0},{2,1},{3,2},{5,4},{6,5},{7,6},{9,8},{10,9},{11,10},{13,12},{... | collective-permute-start | bytes 49160 | tf_op jit(solution)/shard_map/ppermute | solution.py:22
  140.5 4.2 %collective-permute-start.13 = (f32[1,1,32,128]{3,2,1,0:T(8,128)S(1)}, f32[1,1,32,128]{3,2,1,0:T(8,128)S(1)}, u32[]{:S(2)}, u32[]{:S(2)}) collective-permute-start(f32[1,1,32,128]{3,2,1,0:T(8,128)S(1)} %get-tuple-element.80), channel_id=1, source_target_pairs={{1,0},{2,1},{3,2},{5,4},{6,5},{7,6},{9,8},{10,9},{11,10},{13,12},{... | collective-permute-start | bytes 49160 | tf_op jit(solution)/shard_map/ppermute | solution.py:22
  146.0 4.6 %collective-permute-start.21 = (f32[1,1,32,128]{3,2,1,0:T(8,128)S(1)}, f32[1,1,32,128]{3,2,1,0:T(8,128)S(1)}, u32[]{:S(2)}, u32[]{:S(2)}) collective-permute-start(f32[1,1,32,128]{3,2,1,0:T(8,128)S(1)} %get-tuple-element.116), channel_id=1, source_target_pairs={{1,0},{2,1},{3,2},{5,4},{6,5},{7,6},{9,8},{10,9},{11,10},{13,12},{... | collective-permute-start | bytes 49160 | tf_op jit(solution)/shard_map/ppermute | solution.py:22
  152.2 4.1 %collective-permute-done.22 = f32[1,1,32,128]{3,2,1,0:T(8,128)S(1)} collective-permute-done((f32[1,1,32,128]{3,2,1,0:T(8,128)S(1)}, f32[1,1,32,128]{3,2,1,0:T(8,128)S(1)}, u32[]{:S(2)}, u32[]{:S(2)}) %collective-permute-start.22) | collective-permute-done | bytes 16416 | tf_op jit(solution)/shard_map/ppermute | solution.py:20
  156.7 3.8 %collective-permute-start.15 = (f32[1,1,32,128]{3,2,1,0:T(8,128)S(1)}, f32[1,1,32,128]{3,2,1,0:T(8,128)S(1)}, u32[]{:S(2)}, u32[]{:S(2)}) collective-permute-start(f32[1,1,32,128]{3,2,1,0:T(8,128)S(1)} %get-tuple-element.74), channel_id=1, source_target_pairs={{1,0},{2,1},{3,2},{5,4},{6,5},{7,6},{9,8},{10,9},{11,10},{13,12},{... | collective-permute-start | bytes 49160 | tf_op jit(solution)/shard_map/ppermute | solution.py:22
  161.8 4.5 %collective-permute-start.23 = (f32[1,1,32,128]{3,2,1,0:T(8,128)S(1)}, f32[1,1,32,128]{3,2,1,0:T(8,128)S(1)}, u32[]{:S(2)}, u32[]{:S(2)}) collective-permute-start(f32[1,1,32,128]{3,2,1,0:T(8,128)S(1)} %get-tuple-element.110), channel_id=1, source_target_pairs={{1,0},{2,1},{3,2},{5,4},{6,5},{7,6},{9,8},{10,9},{11,10},{13,12},{... | collective-permute-start | bytes 49160 | tf_op jit(solution)/shard_map/ppermute | solution.py:22
  168.0 3.9 %collective-permute-done.24 = f32[1,1,32,128]{3,2,1,0:T(8,128)S(1)} collective-permute-done((f32[1,1,32,128]{3,2,1,0:T(8,128)S(1)}, f32[1,1,32,128]{3,2,1,0:T(8,128)S(1)}, u32[]{:S(2)}, u32[]{:S(2)}) %collective-permute-start.24) | collective-permute-done | bytes 16416 | tf_op jit(solution)/shard_map/ppermute | solution.py:20
  172.3 1.9 collective-permute-start.17
  175.5 4.5 %collective-permute-start.25 = (f32[1,1,32,128]{3,2,1,0:T(8,128)S(1)}, f32[1,1,32,128]{3,2,1,0:T(8,128)S(1)}, u32[]{:S(2)}, u32[]{:S(2)}) collective-permute-start(f32[1,1,32,128]{3,2,1,0:T(8,128)S(1)} %get-tuple-element.104), channel_id=1, source_target_pairs={{1,0},{2,1},{3,2},{5,4},{6,5},{7,6},{9,8},{10,9},{11,10},{13,12},{... | collective-permute-start | bytes 49160 | tf_op jit(solution)/shard_map/ppermute | solution.py:22
  181.8 4.1 %collective-permute-done.26 = f32[1,1,32,128]{3,2,1,0:T(8,128)S(1)} collective-permute-done((f32[1,1,32,128]{3,2,1,0:T(8,128)S(1)}, f32[1,1,32,128]{3,2,1,0:T(8,128)S(1)}, u32[]{:S(2)}, u32[]{:S(2)}) %collective-permute-start.26) | collective-permute-done | bytes 16416 | tf_op jit(solution)/shard_map/ppermute | solution.py:20
  186.2 1.8 collective-permute-start.27
  189.3 4.5 %collective-permute-start.19 = (f32[1,1,32,128]{3,2,1,0:T(8,128)S(1)}, f32[1,1,32,128]{3,2,1,0:T(8,128)S(1)}, u32[]{:S(2)}, u32[]{:S(2)}) collective-permute-start(f32[1,1,32,128]{3,2,1,0:T(8,128)S(1)} %get-tuple-element.62), channel_id=1, source_target_pairs={{1,0},{2,1},{3,2},{5,4},{6,5},{7,6},{9,8},{10,9},{11,10},{13,12},{... | collective-permute-start | bytes 49160 | tf_op jit(solution)/shard_map/ppermute | solution.py:22
  195.5 4.5 %collective-permute-start.29 = (f32[1,1,32,128]{3,2,1,0:T(8,128)S(1)}, f32[1,1,32,128]{3,2,1,0:T(8,128)S(1)}, u32[]{:S(2)}, u32[]{:S(2)}) collective-permute-start(f32[1,1,32,128]{3,2,1,0:T(8,128)S(1)} %get-tuple-element.92), channel_id=1, source_target_pairs={{1,0},{2,1},{3,2},{5,4},{6,5},{7,6},{9,8},{10,9},{11,10},{13,12},{... | collective-permute-start | bytes 49160 | tf_op jit(solution)/shard_map/ppermute | solution.py:22
  201.7 4.0 %collective-permute-done.30 = f32[1,1,32,128]{3,2,1,0:T(8,128)S(1)} collective-permute-done((f32[1,1,32,128]{3,2,1,0:T(8,128)S(1)}, f32[1,1,32,128]{3,2,1,0:T(8,128)S(1)}, u32[]{:S(2)}, u32[]{:S(2)}) %collective-permute-start.30) | collective-permute-done | bytes 16416 | tf_op jit(solution)/shard_map/ppermute | solution.py:20
  (112 shorter events, 28.7 us)
Async XLA Ops:
  6.5 36.2 %all-gather.4.cloned.1.call-start = ((), (), s32[]{:S(2)}) async-start(), calls=%async_computation | async-start | bytes 1179648 | tf_op jit(solution)/shard_map/all_gather | solution.py:31
  18.1 50.0 %all-gather.6.cloned.1.call-start = ((), (), s32[]{:S(2)}) async-start(), calls=%async_computation.1 | async-start | bytes 1179648 | tf_op jit(solution)/shard_map/all_gather | solution.py:31
  18.9 74.7 %all-gather.8.cloned.1.call-start = ((), (), s32[]{:S(2)}) async-start(), calls=%async_computation.2 | async-start | bytes 1179648 | tf_op jit(solution)/shard_map/all_gather | solution.py:31
  19.7 75.3 %collective-permute-start = (f32[1,32,128]{2,1,0:T(8,128)S(1)}, f32[1,32,128]{2,1,0:T(8,128)S(1)}, u32[]{:S(2)}, u32[]{:S(2)}) collective-permute-start(f32[1,32,128]{2,1,0:T(8,128)S(1)} %slice_bitcast_fusion.1), channel_id=1, source_target_pairs={{0,1},{1,2},{2,3},{4,5},{5,6},{6,7},{8,9},{9,10},{10,11},{12,13},{... | collective-permute-start | bytes 49160 | tf_op jit(solution)/shard_map/ppermute | solution.py:37
  98.4 5.6 %collective-permute-start.2 = (f32[1,1,32,128]{3,2,1,0:T(8,128)S(1)}, f32[1,1,32,128]{3,2,1,0:T(8,128)S(1)}, u32[]{:S(2)}, u32[]{:S(2)}) collective-permute-start(f32[1,1,32,128]{3,2,1,0:T(8,128)S(1)} %get-tuple-element.57), channel_id=1, source_target_pairs={{0,1},{1,2},{2,3},{4,5},{5,6},{6,7},{8,9},{9,10},{10,11},{12,13},{... | collective-permute-start | bytes 49160 | tf_op jit(solution)/shard_map/ppermute | solution.py:20
  104.3 3.9 %collective-permute-start.3 = (f32[1,1,32,128]{3,2,1,0:T(8,128)S(1)}, f32[1,1,32,128]{3,2,1,0:T(8,128)S(1)}, u32[]{:S(2)}, u32[]{:S(2)}) collective-permute-start(f32[1,1,32,128]{3,2,1,0:T(8,128)S(1)} %get-tuple-element.50), channel_id=1, source_target_pairs={{1,0},{2,1},{3,2},{5,4},{6,5},{7,6},{9,8},{10,9},{11,10},{13,12},{... | collective-permute-start | bytes 49160 | tf_op jit(solution)/shard_map/ppermute | solution.py:22
  106.8 5.6 %collective-permute-start.4 = (f32[1,1,32,128]{3,2,1,0:T(8,128)S(1)}, f32[1,1,32,128]{3,2,1,0:T(8,128)S(1)}, u32[]{:S(2)}, u32[]{:S(2)}) collective-permute-start(f32[1,1,32,128]{3,2,1,0:T(8,128)S(1)} %get-tuple-element.51), channel_id=1, source_target_pairs={{0,1},{1,2},{2,3},{4,5},{5,6},{6,7},{8,9},{9,10},{10,11},{12,13},{... | collective-permute-start | bytes 49160 | tf_op jit(solution)/shard_map/ppermute | solution.py:20
  112.7 3.9 %collective-permute-start.5 = (f32[1,1,32,128]{3,2,1,0:T(8,128)S(1)}, f32[1,1,32,128]{3,2,1,0:T(8,128)S(1)}, u32[]{:S(2)}, u32[]{:S(2)}) collective-permute-start(f32[1,1,32,128]{3,2,1,0:T(8,128)S(1)} %get-tuple-element.44), channel_id=1, source_target_pairs={{1,0},{2,1},{3,2},{5,4},{6,5},{7,6},{9,8},{10,9},{11,10},{13,12},{... | collective-permute-start | bytes 49160 | tf_op jit(solution)/shard_map/ppermute | solution.py:22
  115.1 5.6 %collective-permute-start.6 = (f32[1,1,32,128]{3,2,1,0:T(8,128)S(1)}, f32[1,1,32,128]{3,2,1,0:T(8,128)S(1)}, u32[]{:S(2)}, u32[]{:S(2)}) collective-permute-start(f32[1,1,32,128]{3,2,1,0:T(8,128)S(1)} %get-tuple-element.45), channel_id=1, source_target_pairs={{0,1},{1,2},{2,3},{4,5},{5,6},{6,7},{8,9},{9,10},{10,11},{12,13},{... | collective-permute-start | bytes 49160 | tf_op jit(solution)/shard_map/ppermute | solution.py:20
  122.9 5.6 %collective-permute-start.8 = (f32[1,1,32,128]{3,2,1,0:T(8,128)S(1)}, f32[1,1,32,128]{3,2,1,0:T(8,128)S(1)}, u32[]{:S(2)}, u32[]{:S(2)}) collective-permute-start(f32[1,1,32,128]{3,2,1,0:T(8,128)S(1)} %get-tuple-element.39), channel_id=1, source_target_pairs={{0,1},{1,2},{2,3},{4,5},{5,6},{6,7},{8,9},{9,10},{10,11},{12,13},{... | collective-permute-start | bytes 49160 | tf_op jit(solution)/shard_map/ppermute | solution.py:20
  129.0 9.7 %collective-permute-start.11 = (f32[1,1,32,128]{3,2,1,0:T(8,128)S(1)}, f32[1,1,32,128]{3,2,1,0:T(8,128)S(1)}, u32[]{:S(2)}, u32[]{:S(2)}) collective-permute-start(f32[1,1,32,128]{3,2,1,0:T(8,128)S(1)} %get-tuple-element.86), channel_id=1, source_target_pairs={{1,0},{2,1},{3,2},{5,4},{6,5},{7,6},{9,8},{10,9},{11,10},{13,12},{... | collective-permute-start | bytes 49160 | tf_op jit(solution)/shard_map/ppermute | solution.py:22
  130.9 7.8 %collective-permute-start.12 = (f32[1,1,32,128]{3,2,1,0:T(8,128)S(1)}, f32[1,1,32,128]{3,2,1,0:T(8,128)S(1)}, u32[]{:S(2)}, u32[]{:S(2)}) collective-permute-start(f32[1,1,32,128]{3,2,1,0:T(8,128)S(1)} %get-tuple-element.87), channel_id=1, source_target_pairs={{0,1},{1,2},{2,3},{4,5},{5,6},{6,7},{8,9},{9,10},{10,11},{12,13},{... | collective-permute-start | bytes 49160 | tf_op jit(solution)/shard_map/ppermute | solution.py:20
  132.2 6.9 %collective-permute-start.10 = (f32[1,1,32,128]{3,2,1,0:T(8,128)S(1)}, f32[1,1,32,128]{3,2,1,0:T(8,128)S(1)}, u32[]{:S(2)}, u32[]{:S(2)}) collective-permute-start(f32[1,1,32,128]{3,2,1,0:T(8,128)S(1)} %get-tuple-element.33), channel_id=1, source_target_pairs={{0,1},{1,2},{2,3},{4,5},{5,6},{6,7},{8,9},{9,10},{10,11},{12,13},{... | collective-permute-start | bytes 49160 | tf_op jit(solution)/shard_map/ppermute | solution.py:20
  133.5 6.6 %collective-permute-start.9 = (f32[1,1,32,128]{3,2,1,0:T(8,128)S(1)}, f32[1,1,32,128]{3,2,1,0:T(8,128)S(1)}, u32[]{:S(2)}, u32[]{:S(2)}) collective-permute-start(f32[1,1,32,128]{3,2,1,0:T(8,128)S(1)} %get-tuple-element.32), channel_id=1, source_target_pairs={{1,0},{2,1},{3,2},{5,4},{6,5},{7,6},{9,8},{10,9},{11,10},{13,12},{... | collective-permute-start | bytes 49160 | tf_op jit(solution)/shard_map/ppermute | solution.py:22
  140.5 11.4 %collective-permute-start.13 = (f32[1,1,32,128]{3,2,1,0:T(8,128)S(1)}, f32[1,1,32,128]{3,2,1,0:T(8,128)S(1)}, u32[]{:S(2)}, u32[]{:S(2)}) collective-permute-start(f32[1,1,32,128]{3,2,1,0:T(8,128)S(1)} %get-tuple-element.80), channel_id=1, source_target_pairs={{1,0},{2,1},{3,2},{5,4},{6,5},{7,6},{9,8},{10,9},{11,10},{13,12},{... | collective-permute-start | bytes 49160 | tf_op jit(solution)/shard_map/ppermute | solution.py:22
  144.7 7.2 %collective-permute-start.14 = (f32[1,1,32,128]{3,2,1,0:T(8,128)S(1)}, f32[1,1,32,128]{3,2,1,0:T(8,128)S(1)}, u32[]{:S(2)}, u32[]{:S(2)}) collective-permute-start(f32[1,1,32,128]{3,2,1,0:T(8,128)S(1)} %get-tuple-element.81), channel_id=1, source_target_pairs={{0,1},{1,2},{2,3},{4,5},{5,6},{6,7},{8,9},{9,10},{10,11},{12,13},{... | collective-permute-start | bytes 49160 | tf_op jit(solution)/shard_map/ppermute | solution.py:20
  146.0 6.2 %collective-permute-start.21 = (f32[1,1,32,128]{3,2,1,0:T(8,128)S(1)}, f32[1,1,32,128]{3,2,1,0:T(8,128)S(1)}, u32[]{:S(2)}, u32[]{:S(2)}) collective-permute-start(f32[1,1,32,128]{3,2,1,0:T(8,128)S(1)} %get-tuple-element.116), channel_id=1, source_target_pairs={{1,0},{2,1},{3,2},{5,4},{6,5},{7,6},{9,8},{10,9},{11,10},{13,12},{... | collective-permute-start | bytes 49160 | tf_op jit(solution)/shard_map/ppermute | solution.py:22
  150.6 5.8 %collective-permute-start.22 = (f32[1,1,32,128]{3,2,1,0:T(8,128)S(1)}, f32[1,1,32,128]{3,2,1,0:T(8,128)S(1)}, u32[]{:S(2)}, u32[]{:S(2)}) collective-permute-start(f32[1,1,32,128]{3,2,1,0:T(8,128)S(1)} %get-tuple-element.117), channel_id=1, source_target_pairs={{0,1},{1,2},{2,3},{4,5},{5,6},{6,7},{8,9},{9,10},{10,11},{12,13},{... | collective-permute-start | bytes 49160 | tf_op jit(solution)/shard_map/ppermute | solution.py:20
  156.7 11.0 %collective-permute-start.15 = (f32[1,1,32,128]{3,2,1,0:T(8,128)S(1)}, f32[1,1,32,128]{3,2,1,0:T(8,128)S(1)}, u32[]{:S(2)}, u32[]{:S(2)}) collective-permute-start(f32[1,1,32,128]{3,2,1,0:T(8,128)S(1)} %get-tuple-element.74), channel_id=1, source_target_pairs={{1,0},{2,1},{3,2},{5,4},{6,5},{7,6},{9,8},{10,9},{11,10},{13,12},{... | collective-permute-start | bytes 49160 | tf_op jit(solution)/shard_map/ppermute | solution.py:22
  160.5 7.2 %collective-permute-start.16 = (f32[1,1,32,128]{3,2,1,0:T(8,128)S(1)}, f32[1,1,32,128]{3,2,1,0:T(8,128)S(1)}, u32[]{:S(2)}, u32[]{:S(2)}) collective-permute-start(f32[1,1,32,128]{3,2,1,0:T(8,128)S(1)} %get-tuple-element.75), channel_id=1, source_target_pairs={{0,1},{1,2},{2,3},{4,5},{5,6},{6,7},{8,9},{9,10},{10,11},{12,13},{... | collective-permute-start | bytes 49160 | tf_op jit(solution)/shard_map/ppermute | solution.py:20
  161.8 6.2 %collective-permute-start.23 = (f32[1,1,32,128]{3,2,1,0:T(8,128)S(1)}, f32[1,1,32,128]{3,2,1,0:T(8,128)S(1)}, u32[]{:S(2)}, u32[]{:S(2)}) collective-permute-start(f32[1,1,32,128]{3,2,1,0:T(8,128)S(1)} %get-tuple-element.110), channel_id=1, source_target_pairs={{1,0},{2,1},{3,2},{5,4},{6,5},{7,6},{9,8},{10,9},{11,10},{13,12},{... | collective-permute-start | bytes 49160 | tf_op jit(solution)/shard_map/ppermute | solution.py:22
  166.3 5.6 %collective-permute-start.24 = (f32[1,1,32,128]{3,2,1,0:T(8,128)S(1)}, f32[1,1,32,128]{3,2,1,0:T(8,128)S(1)}, u32[]{:S(2)}, u32[]{:S(2)}) collective-permute-start(f32[1,1,32,128]{3,2,1,0:T(8,128)S(1)} %get-tuple-element.111), channel_id=1, source_target_pairs={{0,1},{1,2},{2,3},{4,5},{5,6},{6,7},{8,9},{9,10},{10,11},{12,13},{... | collective-permute-start | bytes 49160 | tf_op jit(solution)/shard_map/ppermute | solution.py:20
  172.3 9.1 %collective-permute-start.17 = (f32[1,1,32,128]{3,2,1,0:T(8,128)S(1)}, f32[1,1,32,128]{3,2,1,0:T(8,128)S(1)}, u32[]{:S(2)}, u32[]{:S(2)}) collective-permute-start(f32[1,1,32,128]{3,2,1,0:T(8,128)S(1)} %get-tuple-element.68), channel_id=1, source_target_pairs={{1,0},{2,1},{3,2},{5,4},{6,5},{7,6},{9,8},{10,9},{11,10},{13,12},{... | collective-permute-start | bytes 49160 | tf_op jit(solution)/shard_map/ppermute | solution.py:22
  174.2 7.2 %collective-permute-start.18 = (f32[1,1,32,128]{3,2,1,0:T(8,128)S(1)}, f32[1,1,32,128]{3,2,1,0:T(8,128)S(1)}, u32[]{:S(2)}, u32[]{:S(2)}) collective-permute-start(f32[1,1,32,128]{3,2,1,0:T(8,128)S(1)} %get-tuple-element.69), channel_id=1, source_target_pairs={{0,1},{1,2},{2,3},{4,5},{5,6},{6,7},{8,9},{9,10},{10,11},{12,13},{... | collective-permute-start | bytes 49160 | tf_op jit(solution)/shard_map/ppermute | solution.py:20
  175.5 6.2 %collective-permute-start.25 = (f32[1,1,32,128]{3,2,1,0:T(8,128)S(1)}, f32[1,1,32,128]{3,2,1,0:T(8,128)S(1)}, u32[]{:S(2)}, u32[]{:S(2)}) collective-permute-start(f32[1,1,32,128]{3,2,1,0:T(8,128)S(1)} %get-tuple-element.104), channel_id=1, source_target_pairs={{1,0},{2,1},{3,2},{5,4},{6,5},{7,6},{9,8},{10,9},{11,10},{13,12},{... | collective-permute-start | bytes 49160 | tf_op jit(solution)/shard_map/ppermute | solution.py:22
  180.1 5.7 %collective-permute-start.26 = (f32[1,1,32,128]{3,2,1,0:T(8,128)S(1)}, f32[1,1,32,128]{3,2,1,0:T(8,128)S(1)}, u32[]{:S(2)}, u32[]{:S(2)}) collective-permute-start(f32[1,1,32,128]{3,2,1,0:T(8,128)S(1)} %get-tuple-element.105), channel_id=1, source_target_pairs={{0,1},{1,2},{2,3},{4,5},{5,6},{6,7},{8,9},{9,10},{10,11},{12,13},{... | collective-permute-start | bytes 49160 | tf_op jit(solution)/shard_map/ppermute | solution.py:20
  186.2 9.0 %collective-permute-start.27 = (f32[1,1,32,128]{3,2,1,0:T(8,128)S(1)}, f32[1,1,32,128]{3,2,1,0:T(8,128)S(1)}, u32[]{:S(2)}, u32[]{:S(2)}) collective-permute-start(f32[1,1,32,128]{3,2,1,0:T(8,128)S(1)} %get-tuple-element.98), channel_id=1, source_target_pairs={{1,0},{2,1},{3,2},{5,4},{6,5},{7,6},{9,8},{10,9},{11,10},{13,12},{... | collective-permute-start | bytes 49160 | tf_op jit(solution)/shard_map/ppermute | solution.py:22
  188.0 7.2 %collective-permute-start.28 = (f32[1,1,32,128]{3,2,1,0:T(8,128)S(1)}, f32[1,1,32,128]{3,2,1,0:T(8,128)S(1)}, u32[]{:S(2)}, u32[]{:S(2)}) collective-permute-start(f32[1,1,32,128]{3,2,1,0:T(8,128)S(1)} %get-tuple-element.99), channel_id=1, source_target_pairs={{0,1},{1,2},{2,3},{4,5},{5,6},{6,7},{8,9},{9,10},{10,11},{12,13},{... | collective-permute-start | bytes 49160 | tf_op jit(solution)/shard_map/ppermute | solution.py:20
  189.3 12.0 %collective-permute-start.19 = (f32[1,1,32,128]{3,2,1,0:T(8,128)S(1)}, f32[1,1,32,128]{3,2,1,0:T(8,128)S(1)}, u32[]{:S(2)}, u32[]{:S(2)}) collective-permute-start(f32[1,1,32,128]{3,2,1,0:T(8,128)S(1)} %get-tuple-element.62), channel_id=1, source_target_pairs={{1,0},{2,1},{3,2},{5,4},{6,5},{7,6},{9,8},{10,9},{11,10},{13,12},{... | collective-permute-start | bytes 49160 | tf_op jit(solution)/shard_map/ppermute | solution.py:22
  193.9 7.5 %collective-permute-start.20 = (f32[1,1,32,128]{3,2,1,0:T(8,128)S(1)}, f32[1,1,32,128]{3,2,1,0:T(8,128)S(1)}, u32[]{:S(2)}, u32[]{:S(2)}) collective-permute-start(f32[1,1,32,128]{3,2,1,0:T(8,128)S(1)} %get-tuple-element.63), channel_id=1, source_target_pairs={{0,1},{1,2},{2,3},{4,5},{5,6},{6,7},{8,9},{9,10},{10,11},{12,13},{... | collective-permute-start | bytes 49160 | tf_op jit(solution)/shard_map/ppermute | solution.py:20
  195.5 6.2 %collective-permute-start.29 = (f32[1,1,32,128]{3,2,1,0:T(8,128)S(1)}, f32[1,1,32,128]{3,2,1,0:T(8,128)S(1)}, u32[]{:S(2)}, u32[]{:S(2)}) collective-permute-start(f32[1,1,32,128]{3,2,1,0:T(8,128)S(1)} %get-tuple-element.92), channel_id=1, source_target_pairs={{1,0},{2,1},{3,2},{5,4},{6,5},{7,6},{9,8},{10,9},{11,10},{13,12},{... | collective-permute-start | bytes 49160 | tf_op jit(solution)/shard_map/ppermute | solution.py:22
  200.0 5.6 %collective-permute-start.30 = (f32[1,1,32,128]{3,2,1,0:T(8,128)S(1)}, f32[1,1,32,128]{3,2,1,0:T(8,128)S(1)}, u32[]{:S(2)}, u32[]{:S(2)}) collective-permute-start(f32[1,1,32,128]{3,2,1,0:T(8,128)S(1)} %get-tuple-element.93), channel_id=1, source_target_pairs={{0,1},{1,2},{2,3},{4,5},{5,6},{6,7},{8,9},{9,10},{10,11},{12,13},{... | collective-permute-start | bytes 49160 | tf_op jit(solution)/shard_map/ppermute | solution.py:20
  (4 other events, 9.7 us)
Sparse Core Ops, SparseCore 0:
  18.3 24.4 all-gather.3
  44.7 23.4 all-gather.5
  70.1 23.4 all-gather.7
